TPU v7x, 512 devices: a whole 4x4x16 slice. The times are simulated.
512 devices in a mesh: seq: 64 (over z_lo, y, core), tp: 8 (over z_hi, x).
Axes of the slice: x: 4, y: 4, z: 16 (z_hi: 2, z_lo: 8; z = z_hi * 8 + z_lo), core: 2. Of those that a mesh axis runs over, the one named last changes fastest.
Arguments:
- queries: bfloat16 [16384, 2048], P('seq', 'tp'), may hold values from -42 to 42
- keys: bfloat16 [16384, 2048], P('seq', 'tp'), may hold values from -6.1 to 6.1
- values: bfloat16 [16384, 2048], P('seq', 'tp'), may hold values from -6 to 6
- residual_in: bfloat16 [16384, 2048], P('seq', 'tp'), may hold values from -6 to 6
- bias_table: float32 [16, 32], P('tp'), may hold values from -4 to 4
- buckets: int32 [128, 33], P('seq'), may hold values from 0 to 31
- out_weight: bfloat16 [2048, 2048], P('tp'), may hold values from -0.125 to 0.125
- gate_weight: bfloat16 [2048, 4096], P('seq', 'tp'), may hold values from -0.125 to 0.125
- up_weight: bfloat16 [2048, 4096], P('seq', 'tp'), may hold values from -0.125 to 0.125
- down_weight_t: bfloat16 [2048, 4096], P('seq', 'tp'), may hold values from -0.09375 to 0.09375
- norm_gain: float32 [2048], replicated, may hold values from 0.5 to 1.5
Outputs:
- layer_out: bfloat16 [16384, 2048], P('seq', 'tp')
All inputs are finite; a program needn't handle non-finite values.
Results may differ from a plain program's by a relative error of at most 0.015.
Values may be sent and summed in bfloat16 or wider, within the bound.
A program may use at most 64 MiB of HBM per device.

v0:
```python
import jax
import jax.numpy as jnp
from jax import lax
from jax.sharding import PartitionSpec as P

HEAD_DIM = 128
BUCKETS = 32
TILE = 128
HALF_BAND = 2048
OFFSETS = 33


def shifted(x, axis, by):
    devices = lax.axis_size(axis)
    pairs = [(i, i + by) for i in range(devices) if 0 <= i + by < devices]
    return lax.ppermute(x, axis, pairs)


def attend_local(queries, extended, bucket_blk, table, start, total_len, width):
    rows = queries.shape[0]
    heads = table.shape[0]
    span = rows + 2 * width
    q3 = queries.reshape(rows, heads, HEAD_DIM)
    k3 = extended[0].reshape(span, heads, HEAD_DIM)
    v3 = extended[1].reshape(span, heads, HEAD_DIM)
    scores = jnp.einsum("qhd,khd->hqk", q3, k3, preferred_element_type=jnp.float32) * HEAD_DIM ** (
        -0.5
    )
    tiles_q = rows // TILE
    tiles_k = span // TILE
    onehot = (bucket_blk[:, :, None] == jnp.arange(BUCKETS, dtype=jnp.int32)[None, None, :]).astype(
        jnp.float32
    )
    table_vals = jnp.einsum("qob,hb->hqo", onehot, table, precision=lax.Precision.HIGHEST)
    offset = (
        jnp.arange(tiles_k, dtype=jnp.int32)[None, :]
        - jnp.arange(tiles_q, dtype=jnp.int32)[:, None]
    )
    select = (offset[:, :, None] == jnp.arange(OFFSETS, dtype=jnp.int32)[None, None, :]).astype(
        jnp.float32
    )
    tile_bias = jnp.einsum("qko,hqo->hqk", select, table_vals, precision=lax.Precision.HIGHEST)
    scores = scores.reshape(heads, tiles_q, TILE, tiles_k, TILE) + tile_bias[:, :, None, :, None]
    scores = scores.reshape(heads, rows, span)
    qpos = start + jnp.arange(rows, dtype=jnp.int32)[:, None]
    kpos = start - width + jnp.arange(span, dtype=jnp.int32)[None, :]
    valid = (jnp.abs(qpos - kpos) <= width) & (kpos >= 0) & (kpos < total_len)
    masked = jnp.where(valid[None], scores, -1e30)
    top = jnp.max(masked, axis=-1, keepdims=True)
    expo = jnp.where(valid[None], jnp.exp(masked - top), 0.0)
    weight = (expo / jnp.sum(expo, axis=-1, keepdims=True)).astype(jnp.bfloat16)
    out = jnp.einsum("hqk,khd->qhd", weight, v3, preferred_element_type=jnp.float32)
    return out.astype(jnp.bfloat16).reshape(rows, heads * HEAD_DIM)


def normalize(full_state, norm_gain):
    wide = full_state.astype(jnp.float32)
    scale = lax.rsqrt(jnp.mean(wide * wide, axis=-1, keepdims=True) + 1e-05)
    return (wide * scale * norm_gain).astype(jnp.bfloat16)


def shards(
    queries,
    keys,
    values,
    residual_in,
    bias_table,
    buckets,
    out_weight,
    gate_weight,
    up_weight,
    down_weight_t,
    norm_gain,
):
    rows = queries.shape[0]
    width = HALF_BAND
    reach = width // rows
    paired = jnp.stack([keys, values], 0)
    offsets_list = list(range(reach, 0, -1)) + list(range(-1, -reach - 1, -1))
    arrived = []
    for distance in offsets_list:
        arrived.append(shifted(paired, "seq", distance))
    extended = jnp.concatenate(arrived[:reach] + [paired] + arrived[reach:], axis=1)
    start = lax.axis_index("seq") * rows
    total_len = rows * lax.axis_size("seq")
    attended = attend_local(queries, extended, buckets, bias_table, start, total_len, width)
    partial_value = jnp.dot(attended, out_weight, preferred_element_type=jnp.float32)
    own_sum = lax.psum_scatter(
        partial_value.astype(jnp.bfloat16), "tp", scatter_dimension=1, tiled=True
    ).astype(jnp.float32)
    own_state = (residual_in.astype(jnp.float32) + own_sum).astype(jnp.bfloat16)
    full_state = lax.all_gather(own_state, "tp", axis=1, tiled=True)
    normed = normalize(full_state, norm_gain)
    gate_all, up_all, down_all = (
        lax.all_gather(gate_weight, "seq", axis=0, tiled=True),
        lax.all_gather(up_weight, "seq", axis=0, tiled=True),
        lax.all_gather(down_weight_t, "seq", axis=0, tiled=True),
    )
    gate = jnp.dot(normed, gate_all, preferred_element_type=jnp.float32)
    up = jnp.dot(normed, up_all, preferred_element_type=jnp.float32)
    hidden = (jax.nn.silu(gate) * up).astype(jnp.bfloat16)
    terms = lax.dot_general(
        hidden, down_all, (((1,), (1,)), ((), ())), preferred_element_type=jnp.float32
    )
    ffn_own = lax.psum_scatter(
        terms.astype(jnp.bfloat16), "tp", scatter_dimension=1, tiled=True
    ).astype(jnp.float32)
    return (own_state.astype(jnp.float32) + ffn_own).astype(jnp.bfloat16)


def solution(mesh):
    return jax.shard_map(
        shards,
        mesh=mesh,
        in_specs=(
            P("seq", "tp"),
            P("seq", "tp"),
            P("seq", "tp"),
            P("seq", "tp"),
            P("tp", None),
            P("seq", None),
            P("tp", None),
            P("seq", "tp"),
            P("seq", "tp"),
            P("seq", "tp"),
            P(),
        ),
        out_specs=P("seq", "tp"),
        check_vma=False,
    )
```

profile of v0, /device:TPU:8, one launch (start us, length us, event | category | flops | bytes accessed | tf_op | source)
XLA Modules:
  0.0 815.9 jit_solution(12422391377847241001)
XLA Ops:
  6.5 1.1 copy.16
  7.6 1.0 copy.17
  8.7 4.5 collective-permute-start
  13.2 2.9 collective-permute-start.1
  16.1 4.2 collective-permute-start.2
  20.3 3.7 collective-permute-start.3
  24.0 5.4 collective-permute-start.4
  29.5 0.9 convolution_bitcast_fusion
  30.4 3.7 fusion.4
  34.2 0.2 convolution_bitcast_fusion.1
  34.4 0.1 copy.20
  34.5 5.9 add.69
  40.3 12.3 %add.70 = f32[2,256,4352]{1,2,0:T(8,128)} reshape(f32[2,2,128,34,128]{2,1,4,3,0:T(2,128)} %add.69) | data formatting | bytes 17825792 | tf_op jit(solution)/shard_map/add | solution.py:43
  52.6 2.6 collective-permute-start.5
  55.3 1.0 constant_dynamic-update-slice_fusion.16
  56.3 0.0 collective-permute-done.1
  56.3 4.1 collective-permute-start.6
  60.4 1.0 constant_dynamic-update-slice_fusion.15
  61.3 3.3 collective-permute-start.7
  64.7 2.3 collective-permute-start.8
  67.0 1.9 collective-permute-start.9
  69.0 1.3 collective-permute-start.10
  70.3 1.3 collective-permute-start.11
  71.6 1.3 collective-permute-start.12
  73.0 1.3 collective-permute-start.13
  74.3 5.8 collective-permute-done.9
  80.2 1.3 collective-permute-start.14
  81.5 1.6 collective-permute-done.10
  83.1 1.3 collective-permute-start.15
  84.4 7.0 collective-permute-done.11
  91.4 1.8 collective-permute-done.12
  93.2 17.2 %collective-permute-done.13 = bf16[2,256,256]{1,2,0:T(8,128)(2,1)S(1)} collective-permute-done((bf16[2,256,256]{1,2,0:T(8,128)(2,1)S(1)}, bf16[2,256,256]{1,2,0:T(8,128)(2,1)S(1)}, u32[]{:S(2)}, u32[]{:S(2)}) %collective-permute-start.13) | collective-permute-done | bytes 262176 | tf_op jit(solution)/shard_map/ppermute | solution.py:16
  110.4 3.8 collective-permute-done.14
  114.2 4.0 collective-permute-done.15
  118.3 1.6 fusion.29
  120.0 2.7 copy-done.1
  122.7 2.0 fusion.2
  124.7 5.8 fusion.30
  130.5 4.4 fusion.10
  134.9 0.0 copy-start.7
  135.0 1.5 convolution_convert_fusion.1
  136.4 0.0 reduce-scatter.3.cloned.1.call-update
  136.4 0.2 all-gather.5.cloned.1.call-start
  136.7 117.1 %reduce-scatter.3.cloned.1.call-done = bf16[256,256]{1,0:T(8,128)(2,1)} async-done(((bf16[256,2048]{1,0:T(8,128)(2,1)}), bf16[256,256]{1,0:T(8,128)(2,1)}) %reduce-scatter.3.cloned.1.call-update) | async-done | bytes 131088 | tf_op jit(solution)/shard_map/reduce_scatter | solution.py:88
  253.8 1.6 add_convert_fusion.1
  255.4 0.0 all-gather.5.cloned.1.call-update
  255.4 0.0 all-gather.7.cloned.1.call-start
  255.5 0.7 all-gather.7.cloned.1.call-update
  256.1 0.0 all-gather.11.cloned.1.call-start
  256.2 0.5 all-gather.11.cloned.1.call-update
  256.7 0.0 all-gather.9.cloned.1.call-start
  256.8 0.5 all-gather.9.cloned.1.call-update
  257.3 0.0 reduce-scatter.5.cloned.1.call-start
  257.4 79.4 %all-gather.5.cloned.1.call-done = bf16[256,2048]{1,0:T(8,128)(2,1)} async-done(((bf16[256,256]{1,0:T(8,128)(2,1)}), bf16[256,2048]{1,0:T(8,128)(2,1)}) %all-gather.5.cloned.1.call-update) | async-done | bytes 1048592 | tf_op jit(solution)/shard_map/all_gather | solution.py:92
  336.7 1.6 fusion.6
  338.3 111.6 %all-gather.7.cloned.1.call-done = bf16[2048,512]{1,0:T(8,128)(2,1)} async-done(((bf16[32,512]{1,0:T(8,128)(2,1)}), bf16[2048,512]{1,0:T(8,128)(2,1)}) %all-gather.7.cloned.1.call-update) | async-done | bytes 2097168 | tf_op jit(solution)/shard_map/all_gather | solution.py:95
  450.0 2.7 fusion.18
  452.7 0.0 copy-start.3
  452.7 116.1 %all-gather.11.cloned.1.call-done = bf16[2048,512]{1,0:T(8,128)(2,1)} async-done(((bf16[32,512]{1,0:T(8,128)(2,1)}), bf16[2048,512]{1,0:T(8,128)(2,1)}) %all-gather.11.cloned.1.call-update) | async-done | bytes 2097168 | tf_op jit(solution)/shard_map/all_gather | solution.py:97
  568.7 118.8 %all-gather.9.cloned.1.call-done = bf16[2048,512]{1,0:T(8,128)(2,1)} async-done(((bf16[32,512]{1,0:T(8,128)(2,1)}), bf16[2048,512]{1,0:T(8,128)(2,1)}) %all-gather.9.cloned.1.call-update) | async-done | bytes 2097168 | tf_op jit(solution)/shard_map/all_gather | solution.py:96
  687.5 4.6 convolution_convert_fusion
  692.2 0.0 reduce-scatter.5.cloned.1.call-update
  692.2 115.3 %reduce-scatter.5.cloned.1.call-done = bf16[256,256]{1,0:T(8,128)(2,1)} async-done(((bf16[256,2048]{1,0:T(8,128)(2,1)}), bf16[256,256]{1,0:T(8,128)(2,1)}) %reduce-scatter.5.cloned.1.call-update) | async-done | bytes 131088 | tf_op jit(solution)/shard_map/reduce_scatter | solution.py:105
  807.5 1.6 add_convert_fusion
  (43 shorter events, 0.4 us)
Async XLA Ops:
  6.5 128.4 %copy-start = (bf16[256,2048]{1,0:T(8,128)(2,1)S(1)}, bf16[256,2048]{1,0:T(8,128)(2,1)}, u32[]{:S(2)}) copy-start(bf16[256,2048]{1,0:T(8,128)(2,1)} %param.17) | copy-start | bytes 3145732
  6.5 247.3 %reduce-scatter.3.cloned.1.call-start = ((), (), s32[]{:S(2)}) async-start(), calls=%async_computation.2 | async-start | bytes 1179648 | tf_op jit(solution)/shard_map/reduce_scatter | solution.py:88
  8.7 44.0 %collective-permute-start = (bf16[2,256,256]{1,2,0:T(8,128)(2,1)S(1)}, bf16[2,256,256]{1,2,0:T(8,128)(2,1)}, u32[]{:S(2)}, u32[]{:S(2)}) collective-permute-start(bf16[2,256,256]{1,2,0:T(8,128)(2,1)S(1)} %pad_maximum_fusion), channel_id=1, source_target_pairs={{0,64},{8,72},{16,80},{24,88},{32,96},{40,104},{48,112},{56,120},{... | collective-permute-start | bytes 786440 | tf_op jit(solution)/shard_map/ppermute | solution.py:16
  13.2 43.0 %collective-permute-start.1 = (bf16[2,256,256]{1,2,0:T(8,128)(2,1)S(1)}, bf16[2,256,256]{1,2,0:T(8,128)(2,1)}, u32[]{:S(2)}, u32[]{:S(2)}) collective-permute-start(bf16[2,256,256]{1,2,0:T(8,128)(2,1)S(1)} %pad_maximum_fusion), channel_id=1, source_target_pairs={{0,56},{8,64},{16,72},{24,80},{32,88},{40,96},{48,104},{56,112},{6... | collective-permute-start | bytes 786440 | tf_op jit(solution)/shard_map/ppermute | solution.py:16
  16.1 45.2 %collective-permute-start.2 = (bf16[2,256,256]{1,2,0:T(8,128)(2,1)S(1)}, bf16[2,256,256]{1,2,0:T(8,128)(2,1)S(1)}, u32[]{:S(2)}, u32[]{:S(2)}) collective-permute-start(bf16[2,256,256]{1,2,0:T(8,128)(2,1)S(1)} %pad_maximum_fusion), channel_id=1, source_target_pairs={{0,48},{8,56},{16,64},{24,72},{32,80},{40,88},{48,96},{56,104},{64... | collective-permute-start | bytes 786440 | tf_op jit(solution)/shard_map/ppermute | solution.py:16
  20.3 44.3 %collective-permute-start.3 = (bf16[2,256,256]{1,2,0:T(8,128)(2,1)S(1)}, bf16[2,256,256]{1,2,0:T(8,128)(2,1)S(1)}, u32[]{:S(2)}, u32[]{:S(2)}) collective-permute-start(bf16[2,256,256]{1,2,0:T(8,128)(2,1)S(1)} %pad_maximum_fusion), channel_id=1, source_target_pairs={{0,40},{8,48},{16,56},{24,64},{32,72},{40,80},{48,88},{56,96},{64,... | collective-permute-start | bytes 786440 | tf_op jit(solution)/shard_map/ppermute | solution.py:16
  24.0 43.0 %collective-permute-start.4 = (bf16[2,256,256]{1,2,0:T(8,128)(2,1)S(1)}, bf16[2,256,256]{1,2,0:T(8,128)(2,1)S(1)}, u32[]{:S(2)}, u32[]{:S(2)}) collective-permute-start(bf16[2,256,256]{1,2,0:T(8,128)(2,1)S(1)} %pad_maximum_fusion), channel_id=1, source_target_pairs={{0,32},{8,40},{16,48},{24,56},{32,64},{40,72},{48,80},{56,88},{64,... | collective-permute-start | bytes 786440 | tf_op jit(solution)/shard_map/ppermute | solution.py:16
  52.6 16.3 %collective-permute-start.5 = (bf16[2,256,256]{1,2,0:T(8,128)(2,1)S(1)}, bf16[2,256,256]{1,2,0:T(8,128)(2,1)S(1)}, u32[]{:S(2)}, u32[]{:S(2)}) collective-permute-start(bf16[2,256,256]{1,2,0:T(8,128)(2,1)S(1)} %pad_maximum_fusion), channel_id=1, source_target_pairs={{0,24},{8,32},{16,40},{24,48},{32,56},{40,64},{48,72},{56,80},{64,... | collective-permute-start | bytes 786440 | tf_op jit(solution)/shard_map/ppermute | solution.py:16
  56.3 14.0 %collective-permute-start.6 = (bf16[2,256,256]{1,2,0:T(8,128)(2,1)S(1)}, bf16[2,256,256]{1,2,0:T(8,128)(2,1)S(1)}, u32[]{:S(2)}, u32[]{:S(2)}) collective-permute-start(bf16[2,256,256]{1,2,0:T(8,128)(2,1)S(1)} %pad_maximum_fusion), channel_id=1, source_target_pairs={{0,16},{8,24},{16,32},{24,40},{32,48},{40,56},{48,64},{56,72},{64,... | collective-permute-start | bytes 786440 | tf_op jit(solution)/shard_map/ppermute | solution.py:16
  61.3 10.3 %collective-permute-start.7 = (bf16[2,256,256]{1,2,0:T(8,128)(2,1)S(1)}, bf16[2,256,256]{1,2,0:T(8,128)(2,1)S(1)}, u32[]{:S(2)}, u32[]{:S(2)}) collective-permute-start(bf16[2,256,256]{1,2,0:T(8,128)(2,1)S(1)} %pad_maximum_fusion), channel_id=1, source_target_pairs={{0,8},{8,16},{16,24},{24,32},{32,40},{40,48},{48,56},{56,64},{64,7... | collective-permute-start | bytes 786440 | tf_op jit(solution)/shard_map/ppermute | solution.py:16
  64.7 8.3 %collective-permute-start.8 = (bf16[2,256,256]{1,2,0:T(8,128)(2,1)S(1)}, bf16[2,256,256]{1,2,0:T(8,128)(2,1)S(1)}, u32[]{:S(2)}, u32[]{:S(2)}) collective-permute-start(bf16[2,256,256]{1,2,0:T(8,128)(2,1)S(1)} %pad_maximum_fusion), channel_id=1, source_target_pairs={{8,0},{16,8},{24,16},{32,24},{40,32},{48,40},{56,48},{64,56},{72,6... | collective-permute-start | bytes 786440 | tf_op jit(solution)/shard_map/ppermute | solution.py:16
  67.0 13.2 %collective-permute-start.9 = (bf16[2,256,256]{1,2,0:T(8,128)(2,1)S(1)}, bf16[2,256,256]{1,2,0:T(8,128)(2,1)S(1)}, u32[]{:S(2)}, u32[]{:S(2)}) collective-permute-start(bf16[2,256,256]{1,2,0:T(8,128)(2,1)S(1)} %pad_maximum_fusion), channel_id=1, source_target_pairs={{16,0},{24,8},{32,16},{40,24},{48,32},{56,40},{64,48},{72,56},{80,... | collective-permute-start | bytes 786440 | tf_op jit(solution)/shard_map/ppermute | solution.py:16
  69.0 14.1 %collective-permute-start.10 = (bf16[2,256,256]{1,2,0:T(8,128)(2,1)S(1)}, bf16[2,256,256]{1,2,0:T(8,128)(2,1)S(1)}, u32[]{:S(2)}, u32[]{:S(2)}) collective-permute-start(bf16[2,256,256]{1,2,0:T(8,128)(2,1)S(1)} %pad_maximum_fusion), channel_id=1, source_target_pairs={{24,0},{32,8},{40,16},{48,24},{56,32},{64,40},{72,48},{80,56},{88,... | collective-permute-start | bytes 786440 | tf_op jit(solution)/shard_map/ppermute | solution.py:16
  70.3 21.1 %collective-permute-start.11 = (bf16[2,256,256]{1,2,0:T(8,128)(2,1)S(1)}, bf16[2,256,256]{1,2,0:T(8,128)(2,1)S(1)}, u32[]{:S(2)}, u32[]{:S(2)}) collective-permute-start(bf16[2,256,256]{1,2,0:T(8,128)(2,1)S(1)} %pad_maximum_fusion), channel_id=1, source_target_pairs={{32,0},{40,8},{48,16},{56,24},{64,32},{72,40},{80,48},{88,56},{96,... | collective-permute-start | bytes 786440 | tf_op jit(solution)/shard_map/ppermute | solution.py:16
  71.6 21.6 %collective-permute-start.12 = (bf16[2,256,256]{1,2,0:T(8,128)(2,1)S(1)}, bf16[2,256,256]{1,2,0:T(8,128)(2,1)S(1)}, u32[]{:S(2)}, u32[]{:S(2)}) collective-permute-start(bf16[2,256,256]{1,2,0:T(8,128)(2,1)S(1)} %pad_maximum_fusion), channel_id=1, source_target_pairs={{40,0},{48,8},{56,16},{64,24},{72,32},{80,40},{88,48},{96,56},{104... | collective-permute-start | bytes 786440 | tf_op jit(solution)/shard_map/ppermute | solution.py:16
  73.0 37.4 %collective-permute-start.13 = (bf16[2,256,256]{1,2,0:T(8,128)(2,1)S(1)}, bf16[2,256,256]{1,2,0:T(8,128)(2,1)S(1)}, u32[]{:S(2)}, u32[]{:S(2)}) collective-permute-start(bf16[2,256,256]{1,2,0:T(8,128)(2,1)S(1)} %pad_maximum_fusion), channel_id=1, source_target_pairs={{48,0},{56,8},{64,16},{72,24},{80,32},{88,40},{96,48},{104,56},{11... | collective-permute-start | bytes 786440 | tf_op jit(solution)/shard_map/ppermute | solution.py:16
  80.2 34.0 %collective-permute-start.14 = (bf16[2,256,256]{1,2,0:T(8,128)(2,1)S(1)}, bf16[2,256,256]{1,2,0:T(8,128)(2,1)S(1)}, u32[]{:S(2)}, u32[]{:S(2)}) collective-permute-start(bf16[2,256,256]{1,2,0:T(8,128)(2,1)S(1)} %pad_maximum_fusion), channel_id=1, source_target_pairs={{56,0},{64,8},{72,16},{80,24},{88,32},{96,40},{104,48},{112,56},{1... | collective-permute-start | bytes 786440 | tf_op jit(solution)/shard_map/ppermute | solution.py:16
  83.1 35.2 %collective-permute-start.15 = (bf16[2,256,256]{1,2,0:T(8,128)(2,1)S(1)}, bf16[2,256,256]{1,2,0:T(8,128)(2,1)S(1)}, u32[]{:S(2)}, u32[]{:S(2)}) collective-permute-start(bf16[2,256,256]{1,2,0:T(8,128)(2,1)S(1)} %pad_maximum_fusion), channel_id=1, source_target_pairs={{64,0},{72,8},{80,16},{88,24},{96,32},{104,40},{112,48},{120,56},{... | collective-permute-start | bytes 786440 | tf_op jit(solution)/shard_map/ppermute | solution.py:16
  118.3 1.7 copy-start.5
  118.3 4.4 copy-start.1
  124.7 5.8 copy-start.2
  130.5 123.3 %copy-start.6 = (bf16[256,256]{1,0:T(8,128)(2,1)S(1)}, bf16[256,256]{1,0:T(8,128)(2,1)}, u32[]{:S(2)}) copy-start(bf16[256,256]{1,0:T(8,128)(2,1)} %param.14) | copy-start | bytes 393220
  134.9 315.0 %copy-start.7 = (f32[2048]{0:T(1024)S(1)}, f32[2048]{0:T(1024)}, u32[]{:S(2)}) copy-start(f32[2048]{0:T(1024)} %param.21) | copy-start | bytes 24580
  136.4 200.3 %all-gather.5.cloned.1.call-start = ((), (), s32[]{:S(2)}) async-start(), calls=%async_computation.3 | async-start | bytes 1179648 | tf_op jit(solution)/shard_map/all_gather | solution.py:92
  255.4 194.6 %all-gather.7.cloned.1.call-start = ((), (), s32[]{:S(2)}) async-start(), calls=%async_computation.4 | async-start | bytes 2129920 | tf_op jit(solution)/shard_map/all_gather | solution.py:95
  256.1 312.6 %all-gather.11.cloned.1.call-start = ((), (), s32[]{:S(2)}) async-start(), calls=%async_computation.6 | async-start | bytes 2129920 | tf_op jit(solution)/shard_map/all_gather | solution.py:97
  256.7 430.8 %all-gather.9.cloned.1.call-start = ((), (), s32[]{:S(2)}) async-start(), calls=%async_computation.5 | async-start | bytes 2129920 | tf_op jit(solution)/shard_map/all_gather | solution.py:96
  257.3 550.2 %reduce-scatter.5.cloned.1.call-start = ((), (), s32[]{:S(2)}) async-start(), calls=%async_computation.7 | async-start | bytes 1179648 | tf_op jit(solution)/shard_map/reduce_scatter | solution.py:105
  336.7 350.8 %copy-start.4 = (bf16[256,2048]{1,0:T(8,128)(2,1)S(1)}, bf16[256,2048]{1,0:T(8,128)(2,1)}, u32[]{:S(2)}) copy-start(bf16[256,2048]{1,0:T(8,128)(2,1)} %all-gather.5.cloned.1.call-done) | copy-start | bytes 3145732
  452.7 354.8 %copy-start.3 = (bf16[256,256]{1,0:T(8,128)(2,1)S(1)}, bf16[256,256]{1,0:T(8,128)(2,1)}, u32[]{:S(2)}) copy-start(bf16[256,256]{1,0:T(8,128)(2,1)} %add_convert_fusion.1) | copy-start | bytes 393220
Sparse Core Ops, SparseCore 0:
  136.6 117.1 reduce-scatter.2
  257.3 79.3 all-gather.4
  339.1 110.8 all-gather.6
  452.2 116.4 all-gather.10
  571.0 116.4 all-gather.8
  692.6 114.9 reduce-scatter.4
where the time goes:
time: 817 us; the launch traced here: 816 us
  waiting for transfers between devices  701 us (86%)
  starting transfers between devices  43 us (5%)
  local copies, waits for them, and re-layouts  27 us (3%)
  matrix products  16.3 us (2%)
  other arithmetic  14.4 us (2%)
  between operations  13.9 us (2%)
    all_gather x1, waiting for transfers between devices, shards(): lax.all_gather(up_weight, 'seq', axis=0, tiled=True)  119 us
    reduce_scatter x1, waiting for transfers between devices, shards(): lax.psum_scatter(partial_value.astype(jnp.bfloat16), 'tp', scatter_dimens...  117 us
    all_gather x1, waiting for transfers between devices, shards(): lax.all_gather(down_weight_t, 'seq', axis=0, tiled=True)  116 us
    reduce_scatter x1, waiting for transfers between devices, shards(): lax.psum_scatter(terms.astype(jnp.bfloat16), 'tp', scatter_dimension=1, t...  115 us
    all_gather x1, waiting for transfers between devices, shards(): lax.all_gather(gate_weight, 'seq', axis=0, tiled=True)  112 us
    all_gather x1, waiting for transfers between devices, shards(): full_state = lax.all_gather(own_state, 'tp', axis=1, tiled=True)  79.4 us
    ppermute x16, starting transfers between devices, shifted(): return lax.ppermute(x, axis, pairs)  42.7 us
    ppermute x16, waiting for transfers between devices, shifted(): return lax.ppermute(x, axis, pairs)  41.2 us
  transfers between devices with their start and end apart: 22, of which 13 were waited for; matrix products, arithmetic and copies ran while one was open for 4% of the time, Pallas kernels for 0%

commit v1 on v0

--- a/solution.py
+++ b/solution.py
@@ -89,7 +89,8 @@
         partial_value.astype(jnp.bfloat16), "tp", scatter_dimension=1, tiled=True
     ).astype(jnp.float32)
     own_state = (residual_in.astype(jnp.float32) + own_sum).astype(jnp.bfloat16)
-    full_state = lax.all_gather(own_state, "tp", axis=1, tiled=True)
+    sent = jnp.stack([own_state] * lax.axis_size("tp"))
+    full_state = jnp.concatenate(lax.all_to_all(sent, "tp", 0, 0), axis=1)
     normed = normalize(full_state, norm_gain)
     gate_all, up_all, down_all = (
         lax.all_gather(gate_weight, "seq", axis=0, tiled=True),

time: 817 us -> 673 us (0.82)
  waiting for transfers between devices: 701 us -> 553 us
    all_gather x1, waiting for transfers between devices: 112 us -> 0.03 us  [shards(): lax.all_gather(gate_weight, 'seq', axis=0, tiled=True)]
    all_gather x1 -> x0, waiting for transfers between devices: 79.4 us -> none  [shards(): full_state = lax.all_gather(own_state, 'tp', axis=1, tiled=True)]
    all_to_all x0 -> x1, waiting for transfers between devices: none -> 25.2 us  [shards(): full_state = jnp.concatenate(lax.all_to_all(sent, 'tp', 0, 0), axis=1)]
    all_gather x1, waiting for transfers between devices: 119 us -> 134 us  [shards(): lax.all_gather(up_weight, 'seq', axis=0, tiled=True)]
  transfers between devices with their start and end apart: 22 -> 22, of which waited for: 13 -> 12; matrix products, arithmetic and copies ran while one was open for 4% -> 5% of each run, Pallas kernels for 0% -> 0%
where the time goes in v1:
time: 673 us; the launch traced here: 672 us
  waiting for transfers between devices  553 us (82%)
  starting transfers between devices  46.7 us (7%)
  local copies, waits for them, and re-layouts  28.1 us (4%)
  matrix products  15.9 us (2%)
  between operations  15.5 us (2%)
  other arithmetic  12.8 us (2%)
    all_gather x1, waiting for transfers between devices, shards(): lax.all_gather(up_weight, 'seq', axis=0, tiled=True)  134 us
    all_gather x1, waiting for transfers between devices, shards(): lax.all_gather(down_weight_t, 'seq', axis=0, tiled=True)  119 us
    reduce_scatter x1, waiting for transfers between devices, shards(): lax.psum_scatter(partial_value.astype(jnp.bfloat16), 'tp', scatter_dimens...  117 us
    reduce_scatter x1, waiting for transfers between devices, shards(): lax.psum_scatter(terms.astype(jnp.bfloat16), 'tp', scatter_dimension=1, t...  115 us
    ppermute x16, starting transfers between devices, shifted(): return lax.ppermute(x, axis, pairs)  42.7 us
    ppermute x16, waiting for transfers between devices, shifted(): return lax.ppermute(x, axis, pairs)  41.2 us
    all_to_all x1, waiting for transfers between devices, shards(): full_state = jnp.concatenate(lax.all_to_all(sent, 'tp', 0, 0), axis=1)  25.2 us
    add x2, local copies, waits for them, and re-layouts, attend_local(): scores.reshape(heads, tiles_q, TILE, tiles_k, TILE)  18.2 us
  transfers between devices with their start and end apart: 22, of which 12 were waited for; matrix products, arithmetic and copies ran while one was open for 5% of the time, Pallas kernels for 0%

profile of v1, /device:TPU:8, one launch (start us, length us, event | category | flops | bytes accessed | tf_op | source)
XLA Modules:
  0.0 672.1 jit_solution(17352176545157547694)
XLA Ops:
  7.4 1.1 copy.16
  8.5 1.0 copy.17
  9.5 4.5 collective-permute-start
  14.0 2.9 collective-permute-start.1
  16.9 4.2 collective-permute-start.2
  21.2 3.7 collective-permute-start.3
  24.9 5.4 collective-permute-start.4
  30.3 0.9 convolution_bitcast_fusion
  31.2 3.7 fusion.4
  35.0 0.2 convolution_bitcast_fusion.1
  35.2 0.1 copy.20
  35.3 5.9 add.69
  41.2 12.3 %add.70 = f32[2,256,4352]{1,2,0:T(8,128)} reshape(f32[2,2,128,34,128]{2,1,4,3,0:T(2,128)} %add.69) | data formatting | bytes 17825792 | tf_op jit(solution)/shard_map/add | solution.py:43
  53.5 2.6 collective-permute-start.5
  56.1 1.0 constant_dynamic-update-slice_fusion.16
  57.1 4.1 collective-permute-start.6
  61.2 1.0 constant_dynamic-update-slice_fusion.15
  62.2 3.3 collective-permute-start.7
  65.5 2.3 collective-permute-start.8
  67.8 1.9 collective-permute-start.9
  69.8 1.3 collective-permute-start.10
  71.1 1.3 collective-permute-start.11
  72.5 1.3 collective-permute-start.12
  73.8 1.3 collective-permute-start.13
  75.2 5.8 collective-permute-done.9
  81.0 1.3 collective-permute-start.14
  82.3 1.6 collective-permute-done.10
  83.9 1.3 collective-permute-start.15
  85.2 7.0 %collective-permute-done.11 = bf16[2,256,256]{1,2,0:T(8,128)(2,1)S(1)} collective-permute-done((bf16[2,256,256]{1,2,0:T(8,128)(2,1)S(1)}, bf16[2,256,256]{1,2,0:T(8,128)(2,1)S(1)}, u32[]{:S(2)}, u32[]{:S(2)}) %collective-permute-start.11) | collective-permute-done | bytes 262176 | tf_op jit(solution)/shard_map/ppermute | solution.py:16
  92.2 1.8 collective-permute-done.12
  94.0 17.2 %collective-permute-done.13 = bf16[2,256,256]{1,2,0:T(8,128)(2,1)S(1)} collective-permute-done((bf16[2,256,256]{1,2,0:T(8,128)(2,1)S(1)}, bf16[2,256,256]{1,2,0:T(8,128)(2,1)S(1)}, u32[]{:S(2)}, u32[]{:S(2)}) %collective-permute-start.13) | collective-permute-done | bytes 262176 | tf_op jit(solution)/shard_map/ppermute | solution.py:16
  111.2 3.8 collective-permute-done.14
  115.1 4.0 collective-permute-done.15
  119.1 1.6 fusion.24
  120.8 2.7 copy-done.1
  123.5 2.0 fusion.2
  125.5 5.8 fusion.25
  131.3 4.4 fusion.9
  135.8 0.0 copy-start.5
  135.8 1.5 convolution_convert_fusion.1
  137.3 0.0 reduce-scatter.3.cloned.1.call-update
  137.3 0.0 all-gather.4.cloned.1.call-start
  137.3 0.5 all-gather.4.cloned.1.call-update
  137.9 0.2 all-gather.6.cloned.1.call-start
  138.1 0.4 all-gather.6.cloned.1.call-update
  138.4 116.7 %reduce-scatter.3.cloned.1.call-done = bf16[256,256]{1,0:T(8,128)(2,1)} async-done(((bf16[256,2048]{1,0:T(8,128)(2,1)}), bf16[256,256]{1,0:T(8,128)(2,1)}) %reduce-scatter.3.cloned.1.call-update) | async-done | bytes 131088 | tf_op jit(solution)/shard_map/reduce_scatter | solution.py:88
  255.1 0.9 add_convert_fusion.1
  256.1 0.1 copy.22
  256.2 1.0 stack.11
  257.2 3.7 all-to-all-start
  260.9 0.0 all-gather.8.cloned.1.call-start
  261.0 0.5 all-gather.8.cloned.1.call-update
  261.5 0.0 reduce-scatter.5.cloned.1.call-start
  261.5 25.2 %all-to-all-done = bf16[8,256,256]{1,2,0:T(8,128)(2,1)S(1)} async-done(((bf16[8,256,256]{1,2,0:T(8,128)(2,1)}), bf16[8,256,256]{1,2,0:T(8,128)(2,1)S(1)}, u32[]{:S(2)}, u32[]{:S(2)}) %all-to-all-start) | async-done | bytes 1048608 | tf_op jit(solution)/shard_map/all_to_all | solution.py:93
  286.8 0.3 multiply_reduce_fusion
  287.1 0.3 fusion.7
  287.4 0.0 all-gather.4.cloned.1.call-done
  287.5 2.3 fusion.26
  289.8 134.4 %all-gather.6.cloned.1.call-done = bf16[2048,512]{1,0:T(8,128)(2,1)} async-done(((bf16[32,512]{1,0:T(8,128)(2,1)}), bf16[2048,512]{1,0:T(8,128)(2,1)}) %all-gather.6.cloned.1.call-update) | async-done | bytes 2097168 | tf_op jit(solution)/shard_map/all_gather | solution.py:97
  424.2 119.0 %all-gather.8.cloned.1.call-done = bf16[2048,512]{1,0:T(8,128)(2,1)} async-done(((bf16[32,512]{1,0:T(8,128)(2,1)}), bf16[2048,512]{1,0:T(8,128)(2,1)}) %all-gather.8.cloned.1.call-update) | async-done | bytes 2097168 | tf_op jit(solution)/shard_map/all_gather | solution.py:98
  543.3 4.6 convolution_convert_fusion
  547.8 0.0 reduce-scatter.5.cloned.1.call-update
  547.9 115.0 %reduce-scatter.5.cloned.1.call-done = bf16[256,256]{1,0:T(8,128)(2,1)} async-done(((bf16[256,2048]{1,0:T(8,128)(2,1)}), bf16[256,256]{1,0:T(8,128)(2,1)}) %reduce-scatter.5.cloned.1.call-update) | async-done | bytes 131088 | tf_op jit(solution)/shard_map/reduce_scatter | solution.py:106
  662.9 1.6 add_convert_fusion
  (41 shorter events, 0.4 us)
Async XLA Ops:
  7.4 128.4 %copy-start = (bf16[256,2048]{1,0:T(8,128)(2,1)S(1)}, bf16[256,2048]{1,0:T(8,128)(2,1)}, u32[]{:S(2)}) copy-start(bf16[256,2048]{1,0:T(8,128)(2,1)} %param.17) | copy-start | bytes 3145732
  7.4 247.8 %reduce-scatter.3.cloned.1.call-start = ((), (), s32[]{:S(2)}) async-start(), calls=%async_computation.3 | async-start | bytes 1179648 | tf_op jit(solution)/shard_map/reduce_scatter | solution.py:88
  9.5 44.0 %collective-permute-start = (bf16[2,256,256]{1,2,0:T(8,128)(2,1)S(1)}, bf16[2,256,256]{1,2,0:T(8,128)(2,1)}, u32[]{:S(2)}, u32[]{:S(2)}) collective-permute-start(bf16[2,256,256]{1,2,0:T(8,128)(2,1)S(1)} %pad_maximum_fusion), channel_id=1, source_target_pairs={{0,64},{8,72},{16,80},{24,88},{32,96},{40,104},{48,112},{56,120},{... | collective-permute-start | bytes 786440 | tf_op jit(solution)/shard_map/ppermute | solution.py:16
  14.0 43.1 %collective-permute-start.1 = (bf16[2,256,256]{1,2,0:T(8,128)(2,1)S(1)}, bf16[2,256,256]{1,2,0:T(8,128)(2,1)}, u32[]{:S(2)}, u32[]{:S(2)}) collective-permute-start(bf16[2,256,256]{1,2,0:T(8,128)(2,1)S(1)} %pad_maximum_fusion), channel_id=1, source_target_pairs={{0,56},{8,64},{16,72},{24,80},{32,88},{40,96},{48,104},{56,112},{6... | collective-permute-start | bytes 786440 | tf_op jit(solution)/shard_map/ppermute | solution.py:16
  16.9 45.2 %collective-permute-start.2 = (bf16[2,256,256]{1,2,0:T(8,128)(2,1)S(1)}, bf16[2,256,256]{1,2,0:T(8,128)(2,1)S(1)}, u32[]{:S(2)}, u32[]{:S(2)}) collective-permute-start(bf16[2,256,256]{1,2,0:T(8,128)(2,1)S(1)} %pad_maximum_fusion), channel_id=1, source_target_pairs={{0,48},{8,56},{16,64},{24,72},{32,80},{40,88},{48,96},{56,104},{64... | collective-permute-start | bytes 786440 | tf_op jit(solution)/shard_map/ppermute | solution.py:16
  21.2 44.3 %collective-permute-start.3 = (bf16[2,256,256]{1,2,0:T(8,128)(2,1)S(1)}, bf16[2,256,256]{1,2,0:T(8,128)(2,1)S(1)}, u32[]{:S(2)}, u32[]{:S(2)}) collective-permute-start(bf16[2,256,256]{1,2,0:T(8,128)(2,1)S(1)} %pad_maximum_fusion), channel_id=1, source_target_pairs={{0,40},{8,48},{16,56},{24,64},{32,72},{40,80},{48,88},{56,96},{64,... | collective-permute-start | bytes 786440 | tf_op jit(solution)/shard_map/ppermute | solution.py:16
  24.9 43.0 %collective-permute-start.4 = (bf16[2,256,256]{1,2,0:T(8,128)(2,1)S(1)}, bf16[2,256,256]{1,2,0:T(8,128)(2,1)S(1)}, u32[]{:S(2)}, u32[]{:S(2)}) collective-permute-start(bf16[2,256,256]{1,2,0:T(8,128)(2,1)S(1)} %pad_maximum_fusion), channel_id=1, source_target_pairs={{0,32},{8,40},{16,48},{24,56},{32,64},{40,72},{48,80},{56,88},{64,... | collective-permute-start | bytes 786440 | tf_op jit(solution)/shard_map/ppermute | solution.py:16
  53.5 16.3 %collective-permute-start.5 = (bf16[2,256,256]{1,2,0:T(8,128)(2,1)S(1)}, bf16[2,256,256]{1,2,0:T(8,128)(2,1)S(1)}, u32[]{:S(2)}, u32[]{:S(2)}) collective-permute-start(bf16[2,256,256]{1,2,0:T(8,128)(2,1)S(1)} %pad_maximum_fusion), channel_id=1, source_target_pairs={{0,24},{8,32},{16,40},{24,48},{32,56},{40,64},{48,72},{56,80},{64,... | collective-permute-start | bytes 786440 | tf_op jit(solution)/shard_map/ppermute | solution.py:16
  57.1 14.0 %collective-permute-start.6 = (bf16[2,256,256]{1,2,0:T(8,128)(2,1)S(1)}, bf16[2,256,256]{1,2,0:T(8,128)(2,1)S(1)}, u32[]{:S(2)}, u32[]{:S(2)}) collective-permute-start(bf16[2,256,256]{1,2,0:T(8,128)(2,1)S(1)} %pad_maximum_fusion), channel_id=1, source_target_pairs={{0,16},{8,24},{16,32},{24,40},{32,48},{40,56},{48,64},{56,72},{64,... | collective-permute-start | bytes 786440 | tf_op jit(solution)/shard_map/ppermute | solution.py:16
  62.2 10.3 %collective-permute-start.7 = (bf16[2,256,256]{1,2,0:T(8,128)(2,1)S(1)}, bf16[2,256,256]{1,2,0:T(8,128)(2,1)S(1)}, u32[]{:S(2)}, u32[]{:S(2)}) collective-permute-start(bf16[2,256,256]{1,2,0:T(8,128)(2,1)S(1)} %pad_maximum_fusion), channel_id=1, source_target_pairs={{0,8},{8,16},{16,24},{24,32},{32,40},{40,48},{48,56},{56,64},{64,7... | collective-permute-start | bytes 786440 | tf_op jit(solution)/shard_map/ppermute | solution.py:16
  65.5 8.3 %collective-permute-start.8 = (bf16[2,256,256]{1,2,0:T(8,128)(2,1)S(1)}, bf16[2,256,256]{1,2,0:T(8,128)(2,1)S(1)}, u32[]{:S(2)}, u32[]{:S(2)}) collective-permute-start(bf16[2,256,256]{1,2,0:T(8,128)(2,1)S(1)} %pad_maximum_fusion), channel_id=1, source_target_pairs={{8,0},{16,8},{24,16},{32,24},{40,32},{48,40},{56,48},{64,56},{72,6... | collective-permute-start | bytes 786440 | tf_op jit(solution)/shard_map/ppermute | solution.py:16
  67.8 13.2 %collective-permute-start.9 = (bf16[2,256,256]{1,2,0:T(8,128)(2,1)S(1)}, bf16[2,256,256]{1,2,0:T(8,128)(2,1)S(1)}, u32[]{:S(2)}, u32[]{:S(2)}) collective-permute-start(bf16[2,256,256]{1,2,0:T(8,128)(2,1)S(1)} %pad_maximum_fusion), channel_id=1, source_target_pairs={{16,0},{24,8},{32,16},{40,24},{48,32},{56,40},{64,48},{72,56},{80,... | collective-permute-start | bytes 786440 | tf_op jit(solution)/shard_map/ppermute | solution.py:16
  69.8 14.1 %collective-permute-start.10 = (bf16[2,256,256]{1,2,0:T(8,128)(2,1)S(1)}, bf16[2,256,256]{1,2,0:T(8,128)(2,1)S(1)}, u32[]{:S(2)}, u32[]{:S(2)}) collective-permute-start(bf16[2,256,256]{1,2,0:T(8,128)(2,1)S(1)} %pad_maximum_fusion), channel_id=1, source_target_pairs={{24,0},{32,8},{40,16},{48,24},{56,32},{64,40},{72,48},{80,56},{88,... | collective-permute-start | bytes 786440 | tf_op jit(solution)/shard_map/ppermute | solution.py:16
  71.1 21.1 %collective-permute-start.11 = (bf16[2,256,256]{1,2,0:T(8,128)(2,1)S(1)}, bf16[2,256,256]{1,2,0:T(8,128)(2,1)S(1)}, u32[]{:S(2)}, u32[]{:S(2)}) collective-permute-start(bf16[2,256,256]{1,2,0:T(8,128)(2,1)S(1)} %pad_maximum_fusion), channel_id=1, source_target_pairs={{32,0},{40,8},{48,16},{56,24},{64,32},{72,40},{80,48},{88,56},{96,... | collective-permute-start | bytes 786440 | tf_op jit(solution)/shard_map/ppermute | solution.py:16
  72.5 21.6 %collective-permute-start.12 = (bf16[2,256,256]{1,2,0:T(8,128)(2,1)S(1)}, bf16[2,256,256]{1,2,0:T(8,128)(2,1)S(1)}, u32[]{:S(2)}, u32[]{:S(2)}) collective-permute-start(bf16[2,256,256]{1,2,0:T(8,128)(2,1)S(1)} %pad_maximum_fusion), channel_id=1, source_target_pairs={{40,0},{48,8},{56,16},{64,24},{72,32},{80,40},{88,48},{96,56},{104... | collective-permute-start | bytes 786440 | tf_op jit(solution)/shard_map/ppermute | solution.py:16
  73.8 37.4 %collective-permute-start.13 = (bf16[2,256,256]{1,2,0:T(8,128)(2,1)S(1)}, bf16[2,256,256]{1,2,0:T(8,128)(2,1)S(1)}, u32[]{:S(2)}, u32[]{:S(2)}) collective-permute-start(bf16[2,256,256]{1,2,0:T(8,128)(2,1)S(1)} %pad_maximum_fusion), channel_id=1, source_target_pairs={{48,0},{56,8},{64,16},{72,24},{80,32},{88,40},{96,48},{104,56},{11... | collective-permute-start | bytes 786440 | tf_op jit(solution)/shard_map/ppermute | solution.py:16
  81.0 34.0 %collective-permute-start.14 = (bf16[2,256,256]{1,2,0:T(8,128)(2,1)S(1)}, bf16[2,256,256]{1,2,0:T(8,128)(2,1)S(1)}, u32[]{:S(2)}, u32[]{:S(2)}) collective-permute-start(bf16[2,256,256]{1,2,0:T(8,128)(2,1)S(1)} %pad_maximum_fusion), channel_id=1, source_target_pairs={{56,0},{64,8},{72,16},{80,24},{88,32},{96,40},{104,48},{112,56},{1... | collective-permute-start | bytes 786440 | tf_op jit(solution)/shard_map/ppermute | solution.py:16
  83.9 35.2 %collective-permute-start.15 = (bf16[2,256,256]{1,2,0:T(8,128)(2,1)S(1)}, bf16[2,256,256]{1,2,0:T(8,128)(2,1)S(1)}, u32[]{:S(2)}, u32[]{:S(2)}) collective-permute-start(bf16[2,256,256]{1,2,0:T(8,128)(2,1)S(1)} %pad_maximum_fusion), channel_id=1, source_target_pairs={{64,0},{72,8},{80,16},{88,24},{96,32},{104,40},{112,48},{120,56},{... | collective-permute-start | bytes 786440 | tf_op jit(solution)/shard_map/ppermute | solution.py:16
  119.1 1.7 copy-start.3
  119.1 4.4 copy-start.1
  125.5 5.8 copy-start.2
  131.3 123.8 %copy-start.4 = (bf16[256,256]{1,0:T(8,128)(2,1)S(1)}, bf16[256,256]{1,0:T(8,128)(2,1)}, u32[]{:S(2)}) copy-start(bf16[256,256]{1,0:T(8,128)(2,1)} %param.14) | copy-start | bytes 393220
  135.8 151.3 %copy-start.5 = (f32[2048]{0:T(1024)S(1)}, f32[2048]{0:T(1024)}, u32[]{:S(2)}) copy-start(f32[2048]{0:T(1024)} %param.21) | copy-start | bytes 24580
  137.3 150.2 %all-gather.4.cloned.1.call-start = ((), (), s32[]{:S(2)}) async-start(), calls=%async_computation.4 | async-start | bytes 2129920 | tf_op jit(solution)/shard_map/all_gather | solution.py:96
  137.9 286.3 %all-gather.6.cloned.1.call-start = ((), (), s32[]{:S(2)}) async-start(), calls=%async_computation.5 | async-start | bytes 2129920 | tf_op jit(solution)/shard_map/all_gather | solution.py:97
  257.2 29.6 %all-to-all-start = ((bf16[8,256,256]{1,2,0:T(8,128)(2,1)}), bf16[8,256,256]{1,2,0:T(8,128)(2,1)S(1)}, u32[]{:S(2)}, u32[]{:S(2)}) async-start(bf16[8,256,256]{1,2,0:T(8,128)(2,1)} %stack.11), calls=%async_computation.1 | async-start | bytes 2097152 | tf_op jit(solution)/shard_map/all_to_all | solution.py:93
  260.9 282.3 %all-gather.8.cloned.1.call-start = ((), (), s32[]{:S(2)}) async-start(), calls=%async_computation.6 | async-start | bytes 2129920 | tf_op jit(solution)/shard_map/all_gather | solution.py:98
  261.5 401.4 %reduce-scatter.5.cloned.1.call-start = ((), (), s32[]{:S(2)}) async-start(), calls=%async_computation.7 | async-start | bytes 1179648 | tf_op jit(solution)/shard_map/reduce_scatter | solution.py:106
Sparse Core Ops, SparseCore 0:
  137.4 117.6 reduce-scatter.2
  548.0 114.8 reduce-scatter.4
Sparse Core Ops, SparseCore 1:
  140.1 131.9 all-gather.3
  274.4 149.8 all-gather.5
  426.5 116.7 all-gather.7
